TPU v7x, 512 devices: a whole 4x4x16 slice. The times are simulated.
512 devices in a mesh: dp: 64 (over z, x_lo, core), seq: 8 (over x_hi, y).
Axes of the slice: x: 4 (x_hi: 2, x_lo: 2; x = x_hi * 2 + x_lo), y: 4, z: 16, core: 2. Of those that a mesh axis runs over, the one named last changes fastest.
Arguments:
- queries: bfloat16 [65536, 3072], P(('dp', 'seq')), may hold values from -6 to 6
- key_states: bfloat16 [65536, 3072], P(('dp', 'seq')), may hold values from -6 to 6
- value_states: bfloat16 [65536, 3072], P(('dp', 'seq')), may hold values from -6 to 6
- grad_out: bfloat16 [65536, 2560], P(('dp', 'seq')), may hold values from -24 to 24
- out_weight: bfloat16 [3072, 2560], P('seq', 'dp'), may hold values from -0.109375 to 0.109375
- key_blocks: int32 [24, 16, 16], replicated, may hold values from 0 to 15, as said below
- key_count: int32 [24, 16], replicated, may hold values from 5 to 16
Outputs:
- grad_queries: bfloat16 [65536, 3072], P(('dp', 'seq'))
- grad_keys: bfloat16 [65536, 3072], P(('dp', 'seq'))
- grad_weight: float32 [3072, 2560], P('seq', 'dp')
Inputs may be any that keep to these rules, and one draw needn't show every extreme that they name: The first key_count[h, b] entries of key_blocks[h, b] name distinct key blocks; later entries name the other blocks and are not used. Query blocks 0 and 15 attend all 16 blocks; every other query block attends at most 8 blocks, and some reach 8 for every head.
All inputs are finite; a program needn't handle non-finite values.
Results may differ from a plain program's by a relative error of at most 0.0079.
Values may be sent and summed in bfloat16 or wider, within the bound.
A program may use at most 64 MiB of HBM per device.

v0:
```python
import jax
import jax.numpy as jnp
from jax import lax
from jax.sharding import PartitionSpec as P

HEADS = 24
HD = 128
BLK = 64
RANDB = 3


def forward_rows(query_rows, key_rows, value_rows, live_keys):
    scores = jnp.einsum(
        "rqd,rkd->rqk", query_rows, key_rows, preferred_element_type=jnp.float32
    ) * HD ** (-0.5)
    if live_keys is not None:
        scores = jnp.where(live_keys[:, None, :], scores, -jnp.inf)
    row_max = jnp.max(scores, axis=-1, keepdims=True)
    expo = jnp.exp(scores - row_max)
    probs = expo / jnp.sum(expo, axis=-1, keepdims=True)
    head_out = jnp.einsum(
        "rqk,rkd->rqd", probs.astype(jnp.bfloat16), value_rows, preferred_element_type=jnp.float32
    )
    return (probs, head_out.astype(jnp.bfloat16))


def backward_rows(query_rows, key_rows, value_rows, grad_rows, probs):
    dprob = jnp.einsum("rqd,rkd->rqk", grad_rows, value_rows, preferred_element_type=jnp.float32)
    row_delta = jnp.sum(probs * dprob, axis=-1, keepdims=True)
    dscore = (probs * (dprob - row_delta) * HD ** (-0.5)).astype(jnp.bfloat16)
    grad_q = jnp.einsum("rqk,rkd->rqd", dscore, key_rows, preferred_element_type=jnp.float32)
    grad_k = jnp.einsum("rqk,rqd->rkd", dscore, query_rows, preferred_element_type=jnp.float32)
    return (grad_q, grad_k)


def arrange(head_item):
    query_head, key_head, value_head, grad_head, block_list, block_count = head_item
    seq_length = query_head.shape[0]
    block_total = seq_length // BLK
    slot_count = min(block_total, 5 + RANDB)
    middle = block_total - 2
    query_blocks = query_head.reshape(block_total, BLK, HD)
    key_blocks_here = key_head.reshape(block_total, BLK, HD)
    value_blocks = value_head.reshape(block_total, BLK, HD)
    grad_blocks = grad_head.reshape(block_total, BLK, HD)
    chosen = block_list[1 : block_total - 1, :slot_count]
    live_keys = jnp.repeat(
        jnp.arange(slot_count)[None, :] < block_count[1 : block_total - 1, None], BLK, axis=1
    )
    mid_keys = key_blocks_here[chosen].reshape(middle, slot_count * BLK, HD)
    mid_values = value_blocks[chosen].reshape(middle, slot_count * BLK, HD)
    middle_group = (
        query_blocks[1 : block_total - 1],
        mid_keys,
        mid_values,
        grad_blocks[1 : block_total - 1],
        live_keys,
    )
    edge_queries = jnp.stack((query_blocks[0], query_blocks[block_total - 1]))
    edge_grads = jnp.stack((grad_blocks[0], grad_blocks[block_total - 1]))
    edge_keys = jnp.broadcast_to(key_head[None], (2, seq_length, HD))
    edge_values = jnp.broadcast_to(value_head[None], (2, seq_length, HD))
    edge_group = (edge_queries, edge_keys, edge_values, edge_grads, None)
    return (middle_group, edge_group, chosen)


def join_rows(edge_part, middle_part):
    return jnp.concatenate((edge_part[:1], middle_part, edge_part[1:]), axis=0).reshape(-1, HD)


def attend_full(head_item):
    middle_group, edge_group, chosen = arrange(head_item)
    mid_probs, mid_out = forward_rows(
        middle_group[0], middle_group[1], middle_group[2], middle_group[4]
    )
    edge_probs, edge_out = forward_rows(edge_group[0], edge_group[1], edge_group[2], None)
    mid_dq, mid_dk = backward_rows(
        middle_group[0], middle_group[1], middle_group[2], middle_group[3], mid_probs
    )
    edge_dq, edge_dk = backward_rows(
        edge_group[0], edge_group[1], edge_group[2], edge_group[3], edge_probs
    )
    block_total = head_item[0].shape[0] // BLK
    slot_count = chosen.shape[1]
    spread = (chosen[:, :, None] == jnp.arange(block_total)[None, None, :]).astype(jnp.float32)
    key_sum = jnp.einsum(
        "msn,msbd->nbd",
        spread,
        mid_dk.reshape(chosen.shape[0], slot_count, BLK, HD),
        precision=lax.Precision.HIGHEST,
    ).reshape(-1, HD)
    key_sum = key_sum + jnp.sum(edge_dk, axis=0)
    grad_query = join_rows(edge_dq, mid_dq).astype(jnp.bfloat16)
    return (join_rows(edge_out, mid_out), grad_query, key_sum.astype(jnp.bfloat16))


def project_back(whole_grad, out_weight):
    whole_rows = lax.all_gather(out_weight, "dp", axis=1, tiled=True)
    return lax.dot_general(
        whole_grad, whole_rows, (((1,), (1,)), ((), ())), preferred_element_type=jnp.float32
    )


def reduce_grads(head_outputs, whole_grad):
    local_count = head_outputs.shape[0]
    local_sum = jnp.einsum(
        "hld,lc->hdc", head_outputs, whole_grad, preferred_element_type=jnp.float32
    )
    local_sum = local_sum.reshape(local_count * HD, whole_grad.shape[1])
    return lax.psum_scatter(local_sum, "dp", scatter_dimension=1, tiled=True)


def per_device(queries, key_states, value_states, grad_out, out_weight, key_blocks, key_count):
    group_size = lax.axis_size("seq")
    local_heads = HEADS // group_size
    query_all, key_all, value_all = (
        lax.all_to_all(queries, "seq", split_axis=1, concat_axis=0, tiled=True),
        lax.all_to_all(key_states, "seq", split_axis=1, concat_axis=0, tiled=True),
        lax.all_to_all(value_states, "seq", split_axis=1, concat_axis=0, tiled=True),
    )
    whole_grad = lax.all_gather(grad_out, "seq", axis=0, tiled=True)
    seq_length = query_all.shape[0]
    first_head = lax.axis_index("seq") * local_heads
    lists_here = lax.dynamic_slice_in_dim(key_blocks, first_head, local_heads, 0)
    counts_here = lax.dynamic_slice_in_dim(key_count, first_head, local_heads, 0)
    grad_heads = project_back(whole_grad, out_weight).astype(jnp.bfloat16)

    def split_heads(array_in):
        return array_in.reshape(seq_length, local_heads, HD).transpose(1, 0, 2)

    def merge_heads(array_in):
        return array_in.transpose(1, 0, 2).reshape(seq_length, local_heads * HD)

    stacked = (
        split_heads(query_all),
        split_heads(key_all),
        split_heads(value_all),
        split_heads(grad_heads),
        lists_here,
        counts_here,
    )
    head_outputs, grad_q, grad_k = lax.map(attend_full, stacked)
    weight_part = reduce_grads(head_outputs, whole_grad)
    grad_queries, grad_keys = (
        lax.all_to_all(merge_heads(grad_q), "seq", split_axis=0, concat_axis=1, tiled=True),
        lax.all_to_all(merge_heads(grad_k), "seq", split_axis=0, concat_axis=1, tiled=True),
    )
    return (grad_queries, grad_keys, weight_part)


def solution(mesh):
    return jax.shard_map(
        per_device,
        mesh=mesh,
        in_specs=(
            P(("dp", "seq"), None),
            P(("dp", "seq"), None),
            P(("dp", "seq"), None),
            P(("dp", "seq"), None),
            P("seq", "dp"),
            P(),
            P(),
        ),
        out_specs=(P(("dp", "seq"), None), P(("dp", "seq"), None), P("seq", "dp")),
        check_vma=False,
    )
```

profile of v0, /device:TPU:1, one launch (start us, length us, event | category | flops | bytes accessed | tf_op | source)
XLA Modules:
  0.0 637.1 jit_solution(14986661294399659930)
XLA Ops:
  11.0 7.5 %all-to-all-start = ((bf16[128,8,384]{0,2,1:T(8,128)(2,1)}), bf16[128,8,384]{0,2,1:T(8,128)(2,1)S(1)}, u32[]{:S(2)}, u32[]{:S(2)}) async-start(bf16[128,8,384]{0,2,1:T(8,128)(2,1)} %bitcast.19), calls=%async_computation | async-start | bytes 1572864 | tf_op jit(solution)/shard_map/all_to_all | solution.py:117
  19.6 8.7 %all-to-all-done = bf16[128,8,384]{0,2,1:T(8,128)(2,1)S(1)} async-done(((bf16[128,8,384]{0,2,1:T(8,128)(2,1)}), bf16[128,8,384]{0,2,1:T(8,128)(2,1)S(1)}, u32[]{:S(2)}, u32[]{:S(2)}) %all-to-all-start) | async-done | bytes 786464 | tf_op jit(solution)/shard_map/all_to_all | solution.py:117
  28.3 6.6 %all-to-all-start.1 = ((bf16[128,8,384]{0,2,1:T(8,128)(2,1)}), bf16[128,8,384]{0,2,1:T(8,128)(2,1)S(1)}, u32[]{:S(2)}, u32[]{:S(2)}) async-start(bf16[128,8,384]{0,2,1:T(8,128)(2,1)} %bitcast.22), calls=%async_computation.1 | async-start | bytes 1572864 | tf_op jit(solution)/shard_map/all_to_all | solution.py:118
  36.2 10.6 %all-to-all-done.1 = bf16[128,8,384]{0,2,1:T(8,128)(2,1)S(1)} async-done(((bf16[128,8,384]{0,2,1:T(8,128)(2,1)}), bf16[128,8,384]{0,2,1:T(8,128)(2,1)S(1)}, u32[]{:S(2)}, u32[]{:S(2)}) %all-to-all-start.1) | async-done | bytes 786464 | tf_op jit(solution)/shard_map/all_to_all | solution.py:118
  46.8 5.4 all-to-all-start.2
  55.9 7.9 %all-to-all-done.2 = bf16[128,8,384]{0,2,1:T(8,128)(2,1)S(1)} async-done(((bf16[128,8,384]{0,2,1:T(8,128)(2,1)}), bf16[128,8,384]{0,2,1:T(8,128)(2,1)S(1)}, u32[]{:S(2)}, u32[]{:S(2)}) %all-to-all-start.2) | async-done | bytes 786464 | tf_op jit(solution)/shard_map/all_to_all | solution.py:119
  65.6 72.3 %all-gather.5.cloned.1.call-done = bf16[384,2560]{0,1:T(8,128)(2,1)} async-done(((bf16[384,40]{0,1:T(8,128)(2,1)}), bf16[384,2560]{0,1:T(8,128)(2,1)}) %all-gather.5.cloned.1.call-update) | async-done | bytes 1966096 | tf_op jit(solution)/shard_map/all_gather | solution.py:98
  138.0 94.1 %all-gather.3.cloned.1.call-done = bf16[1024,2560]{1,0:T(8,128)(2,1)} async-done(((bf16[128,2560]{1,0:T(8,128)(2,1)}), bf16[1024,2560]{1,0:T(8,128)(2,1)}) %all-gather.3.cloned.1.call-update) | async-done | bytes 5242896 | tf_op jit(solution)/shard_map/all_gather | solution.py:121
  232.1 5.3 convolution_convert_fusion.3
  238.6 152.2 %while.14 = (s32[]{:T(128)}, bf16[3,1024,128]{2,1,0:T(8,128)(2,1)}, bf16[3,1024,128]{2,1,0:T(8,128)(2,1)}, bf16[3,1024,128]{2,1,0:T(8,128)(2,1)}, bf16[3,1024,12...) while((s32[]{:T(128)}, bf16[3,1024,128]{2,1,0:T(8,128)(2,1)}, ...), condition=%wide.region_7.8_spmd, body=%wide.region_0.7_spmd.sunk | while | flops 979120320 | bytes 70489952 | solution.py:142
  250.0 3.5 fusion.160
  256.0 3.7 convolution_convert_fusion.9
  259.8 8.7 %fusion.163 = bf16[14,64,128]{2,1,0:T(8,128)(2,1)} fusion(bf16[14,512,128]{2,1,0:T(8,128)(2,1)S(1)} %bitcast.145, f32[14,64,512]{2,1,0:T(8,128)} %fusion.160, f32[14,64,512]{2,1,0:T(8,128)} %get-tuple-element.217, f32[14,64]{1,0:T(8,128)S(1)} %get-tuple-element.218), kind=kOutput, calls=%fused_computation.27.clone.1 | convolution fusion | flops 120767872 | bytes 5737984 | tf_op jit(solution)/shard_map/while/body/eval_jaxpr/rqk,rkd->rqd/dot_general | solution.py:31
  268.5 10.8 %fusion.165 = f32[14,512,128]{2,1,0:T(8,128)} fusion(bf16[14,64,128]{2,1,0:T(8,128)(2,1)S(1)} %bitcast.152, f32[14,64,512]{2,1,0:T(8,128)} %fusion.160, f32[14,64,512]{2,1,0:T(8,128)} %get-tuple-element.217, f32[14,64]{1,0:T(8,128)S(1)} %get-tuple-element.218), kind=kOutput, calls=%fused_computation.14.clone.1 | convolution fusion | flops 120653184 | bytes 7572992 | tf_op jit(solution)/shard_map/while/body/eval_jaxpr/rqk,rqd->rkd/dot_general | solution.py:32
  279.3 6.1 fusion.166
  300.7 3.5 fusion.160
  306.7 3.7 convolution_convert_fusion.9
  310.5 8.7 %fusion.163 = bf16[14,64,128]{2,1,0:T(8,128)(2,1)} fusion(bf16[14,512,128]{2,1,0:T(8,128)(2,1)S(1)} %bitcast.145, f32[14,64,512]{2,1,0:T(8,128)} %fusion.160, f32[14,64,512]{2,1,0:T(8,128)} %get-tuple-element.217, f32[14,64]{1,0:T(8,128)S(1)} %get-tuple-element.218), kind=kOutput, calls=%fused_computation.27.clone.1 | convolution fusion | flops 120767872 | bytes 5737984 | tf_op jit(solution)/shard_map/while/body/eval_jaxpr/rqk,rkd->rqd/dot_general | solution.py:31
  319.2 10.8 %fusion.165 = f32[14,512,128]{2,1,0:T(8,128)} fusion(bf16[14,64,128]{2,1,0:T(8,128)(2,1)S(1)} %bitcast.152, f32[14,64,512]{2,1,0:T(8,128)} %fusion.160, f32[14,64,512]{2,1,0:T(8,128)} %get-tuple-element.217, f32[14,64]{1,0:T(8,128)S(1)} %get-tuple-element.218), kind=kOutput, calls=%fused_computation.14.clone.1 | convolution fusion | flops 120653184 | bytes 7572992 | tf_op jit(solution)/shard_map/while/body/eval_jaxpr/rqk,rqd->rkd/dot_general | solution.py:32
  330.0 6.1 fusion.166
  351.4 3.5 fusion.160
  357.5 3.7 convolution_convert_fusion.9
  361.2 8.7 %fusion.163 = bf16[14,64,128]{2,1,0:T(8,128)(2,1)} fusion(bf16[14,512,128]{2,1,0:T(8,128)(2,1)S(1)} %bitcast.145, f32[14,64,512]{2,1,0:T(8,128)} %fusion.160, f32[14,64,512]{2,1,0:T(8,128)} %get-tuple-element.217, f32[14,64]{1,0:T(8,128)S(1)} %get-tuple-element.218), kind=kOutput, calls=%fused_computation.27.clone.1 | convolution fusion | flops 120767872 | bytes 5737984 | tf_op jit(solution)/shard_map/while/body/eval_jaxpr/rqk,rkd->rqd/dot_general | solution.py:31
  369.9 10.8 %fusion.165 = f32[14,512,128]{2,1,0:T(8,128)} fusion(bf16[14,64,128]{2,1,0:T(8,128)(2,1)S(1)} %bitcast.152, f32[14,64,512]{2,1,0:T(8,128)} %fusion.160, f32[14,64,512]{2,1,0:T(8,128)} %get-tuple-element.217, f32[14,64]{1,0:T(8,128)S(1)} %get-tuple-element.218), kind=kOutput, calls=%fused_computation.14.clone.1 | convolution fusion | flops 120653184 | bytes 7572992 | tf_op jit(solution)/shard_map/while/body/eval_jaxpr/rqk,rqd->rkd/dot_general | solution.py:32
  380.7 6.1 fusion.166
  390.8 6.9 %fusion.81 = f32[3,128,2560]{2,1,0:T(8,128)} fusion(bf16[3,1024,128]{2,1,0:T(8,128)(2,1)} %get-tuple-element.59, bf16[1024,2560]{1,0:T(8,128)(2,1)} %all-gather.3.cloned.1.call-done), kind=kOutput, calls=%fused_computation.93 | convolution fusion | flops 2013265920 | bytes 9961472 | tf_op jit(solution)/shard_map/hld,lc->hdc/dot_general | solution.py:106
  397.7 5.6 copy.73
  405.8 3.5 all-to-all-start.4
  410.9 9.7 %all-to-all-done.4 = bf16[8,128,384]{1,2,0:T(8,128)(2,1)S(1)} async-done(((bf16[8,128,384]{1,2,0:T(8,128)(2,1)}), bf16[8,128,384]{1,2,0:T(8,128)(2,1)S(1)}, u32[]{:S(2)}, u32[]{:S(2)}) %all-to-all-start.4) | async-done | bytes 786464 | tf_op jit(solution)/shard_map/all_to_all | solution.py:146
  420.6 6.0 all-to-all-start.3
  427.8 12.6 %all-to-all-done.3 = bf16[8,128,384]{1,2,0:T(8,128)(2,1)S(1)} async-done(((bf16[8,128,384]{1,2,0:T(8,128)(2,1)}), bf16[8,128,384]{1,2,0:T(8,128)(2,1)S(1)}, u32[]{:S(2)}, u32[]{:S(2)}) %all-to-all-start.3) | async-done | bytes 786464 | tf_op jit(solution)/shard_map/all_to_all | solution.py:145
  441.5 189.0 %reduce-scatter.5.cloned.1.call-done = f32[384,40]{0,1:T(8,128)} async-done(((f32[384,2560]{0,1:T(8,128)}), f32[384,40]{0,1:T(8,128)}) %reduce-scatter.5.cloned.1.call-update) | async-done | bytes 61456
  (217 shorter events, 72.1 us)
Async XLA Ops:
  7.2 45.2 %copy-start = (s32[24,16,16]{0,2,1:T(8,128)S(1)}, s32[24,16,16]{0,2,1:T(8,128)}, u32[]{:S(2)}) copy-start(s32[24,16,16]{0,2,1:T(8,128)} %param.14) | copy-start | bytes 73732
  7.2 130.8 %all-gather.5.cloned.1.call-start = ((), (), s32[]{:S(2)}) async-start(), calls=%async_computation.7 | async-start | bytes 1996800 | tf_op jit(solution)/shard_map/all_gather | solution.py:98
  7.9 10.5 %copy-start.8 = (bf16[128,3072]{1,0:T(8,128)(2,1)S(1)}, bf16[128,3072]{1,0:T(8,128)(2,1)}, u32[]{:S(2)}) copy-start(bf16[128,3072]{1,0:T(8,128)(2,1)} %param.10) | copy-start | bytes 2359300
  7.9 224.2 %all-gather.3.cloned.1.call-start = ((), (), s32[]{:S(2)}) async-start(), calls=%async_computation.6 | async-start | bytes 5898240 | tf_op jit(solution)/shard_map/all_gather | solution.py:121
  11.0 17.4 %all-to-all-start = ((bf16[128,8,384]{0,2,1:T(8,128)(2,1)}), bf16[128,8,384]{0,2,1:T(8,128)(2,1)S(1)}, u32[]{:S(2)}, u32[]{:S(2)}) async-start(bf16[128,8,384]{0,2,1:T(8,128)(2,1)} %bitcast.19), calls=%async_computation | async-start | bytes 1572864 | tf_op jit(solution)/shard_map/all_to_all | solution.py:117
  18.4 16.5 %copy-start.9 = (bf16[128,3072]{1,0:T(8,128)(2,1)S(1)}, bf16[128,3072]{1,0:T(8,128)(2,1)}, u32[]{:S(2)}) copy-start(bf16[128,3072]{1,0:T(8,128)(2,1)} %param.11) | copy-start | bytes 2359300
  28.3 18.4 %all-to-all-start.1 = ((bf16[128,8,384]{0,2,1:T(8,128)(2,1)}), bf16[128,8,384]{0,2,1:T(8,128)(2,1)S(1)}, u32[]{:S(2)}, u32[]{:S(2)}) async-start(bf16[128,8,384]{0,2,1:T(8,128)(2,1)} %bitcast.22), calls=%async_computation.1 | async-start | bytes 1572864 | tf_op jit(solution)/shard_map/all_to_all | solution.py:118
  35.0 17.2 %copy-start.14 = (s32[24,16]{0,1:T(8,128)S(1)}, s32[24,16]{0,1:T(8,128)}, u32[]{:S(2)}) copy-start(s32[24,16]{0,1:T(8,128)} %param.15) | copy-start | bytes 4612
  46.8 17.1 %all-to-all-start.2 = ((bf16[128,8,384]{0,2,1:T(8,128)(2,1)}), bf16[128,8,384]{0,2,1:T(8,128)(2,1)S(1)}, u32[]{:S(2)}, u32[]{:S(2)}) async-start(bf16[128,8,384]{0,2,1:T(8,128)(2,1)} %bitcast.25), calls=%async_computation.2 | async-start | bytes 1572864 | tf_op jit(solution)/shard_map/all_to_all | solution.py:119
  52.1 578.4 %reduce-scatter.5.cloned.1.call-start = ((), (), s32[]{:S(2)}) async-start(), calls=%async_computation.8 | async-start | bytes 3993600
  238.6 2.1 copy-start.15
  238.6 3.6 copy-start.3
  254.2 1.8 copy-start.1
  279.3 6.3 copy-start.13
  285.4 2.7 copy-start.5
  285.5 2.5 copy-start.6
  285.6 2.5 copy-start.7
  289.3 2.1 copy-start.15
  289.3 3.6 copy-start.3
  330.0 6.3 copy-start.13
  336.1 2.7 copy-start.5
  336.3 2.6 copy-start.6
  336.3 2.6 copy-start.7
  340.1 2.1 copy-start.15
  340.1 3.6 copy-start.3
  380.7 6.3 copy-start.13
  386.8 2.7 copy-start.5
  387.0 2.5 copy-start.6
  387.0 2.5 copy-start.7
  404.8 4.6 copy-start.11
  405.8 14.8 %all-to-all-start.4 = ((bf16[8,128,384]{1,2,0:T(8,128)(2,1)}), bf16[8,128,384]{1,2,0:T(8,128)(2,1)S(1)}, u32[]{:S(2)}, u32[]{:S(2)}) async-start(bf16[8,128,384]{1,2,0:T(8,128)(2,1)} %copy.71), calls=%async_computation.4 | async-start | bytes 1572864 | tf_op jit(solution)/shard_map/all_to_all | solution.py:146
  420.6 19.8 %all-to-all-start.3 = ((bf16[8,128,384]{1,2,0:T(8,128)(2,1)}), bf16[8,128,384]{1,2,0:T(8,128)(2,1)S(1)}, u32[]{:S(2)}, u32[]{:S(2)}) async-start(bf16[8,128,384]{1,2,0:T(8,128)(2,1)} %copy.69), calls=%async_computation.3 | async-start | bytes 1572864 | tf_op jit(solution)/shard_map/all_to_all | solution.py:145
  (15 other events, 18.4 us)
Sparse Core Ops, SparseCore 0:
  10.2 127.7 all-gather.4
  141.1 90.9 all-gather.2
  403.4 227.1 reduce-scatter.4
where the time goes:
time: 642 us; the launch traced here: 637 us
  waiting for transfers between devices  406 us (63%)
  matrix products  126 us (20%)
  local copies, waits for them, and re-layouts  55.3 us (9%)
  starting transfers between devices  29.2 us (5%)
  between operations  13.9 us (2%)
    unnamed x4, waiting for transfers between devices  190 us
    all_gather x1, waiting for transfers between devices, per_device(): whole_grad = lax.all_gather(grad_out, 'seq', axis=0, tiled=True)  94.1 us
    all_gather x1, waiting for transfers between devices, project_back(): whole_rows = lax.all_gather(out_weight, 'dp', axis=1, tiled=True)  72.3 us
    dot_general x6, matrix products, backward_rows(): jnp.einsum('rqk,rqd->rkd', dscore, query_rows, preferred_element_type=jnp...  39.7 us
    dot_general x6, matrix products, backward_rows(): jnp.einsum('rqk,rkd->rqd', dscore, key_rows, preferred_element_type=jnp.f...  27.4 us
    dot_general x3, matrix products, attend_full(): jnp.einsum('msn,msbd->nbd', spread, mid_dk.reshape(chosen.shape[0], slot_...  18.3 us
    dot_general x6, matrix products, forward_rows(): jnp.einsum('rqk,rkd->rqd', probs.astype(jnp.bfloat16), value_rows, prefer...  12.9 us
  transfers between devices with their start and end apart: 8, of which 8 were waited for; matrix products, arithmetic and copies ran while one was open for 2% of the time, Pallas kernels for 0%

commit v1 on v0

v1 whole, which is shorter than its diff:
```python
import functools

import jax
import jax.numpy as jnp
from jax import lax
from jax.experimental import pallas as pl
from jax.experimental.pallas import tpu as pltpu
from jax.sharding import PartitionSpec as P

HEADS = 24
HD = 128
BLK = 64
LOG2E = 1.4426950408889634
MESH = pl.DeviceIdType.MESH

SEQ = 8
ROWS = 128
LEN = SEQ * ROWS
LH = HEADS // SEQ
LW = LH * HD
CW = 2560
HALF = ROWS // 2
ZN = 16
OWN = CW // 64


def dot_nn(a, b):
    return lax.dot_general(a, b, (((1,), (0,)), ((), ())), preferred_element_type=jnp.float32)


def dot_nt(a, b):
    return lax.dot_general(a, b, (((1,), (1,)), ((), ())), preferred_element_type=jnp.float32)


def dot_tn(a, b):
    return lax.dot_general(a, b, (((0,), (0,)), ((), ())), preferred_element_type=jnp.float32)


def kernel(
    q_ref, k_ref, v_ref, g_ref, w_ref, kb_ref,
    dq_out, dk_out, dw_out,
    qg, kg, vg, gall, wbuf, wt, bias, probs, outs, dqb, dkb, dkacc, gw,
    rsrc, r1, t1, r2, t2, r3,
    in_send, in_recv, loc, g_send, g_recv, w_send, w_recv, o_send, o_recv, r_send, r_recv,
):
    dp = lax.axis_index("dp")
    me = lax.axis_index("seq")
    z = dp // 4
    quad = dp % 4
    xl = quad // 2
    core = quad % 2
    xh = me // 4
    y = me % 4

    def seq_at(dx, dy):
        return ((xh + dx) % 2) * 4 + (y + dy) % 4

    peers = [seq_at(dx, dy) for dx, dy in ((0, 1), (0, 3), (1, 0), (0, 2), (1, 1), (1, 3), (1, 2))]
    mate = z * 4 + xl * 2 + (1 - core)
    side = z * 4 + (1 - xl) * 2 + core

    def z_at(d):
        return (z + d) % ZN

    barrier = pltpu.get_barrier_semaphore()
    targets = [(dp, p) for p in peers] + [(mate, me), (side, me)]
    targets += [(z_at(d) * 4 + quad, me) for d in range(1, ZN)]
    for t in targets:
        pl.semaphore_signal(barrier, inc=1, device_id=t, device_id_type=MESH)

    def cols(p):
        return pl.ds(pl.multiple_of(p * LW, 128), LW)

    local = [
        pltpu.make_async_copy(src.at[:, cols(me)], dst.at[me], loc.at[i])
        for i, (src, dst) in enumerate(((q_ref, qg), (k_ref, kg), (v_ref, vg)))
    ]
    local.append(pltpu.make_async_copy(g_ref, gall.at[me], loc.at[3]))
    local.append(pltpu.make_async_copy(w_ref, wbuf.at[quad, z], loc.at[4]))
    for c in local:
        c.start()

    key_block = lax.broadcasted_iota(jnp.int32, (16, LEN), 1) // BLK
    for h in range(LH):
        lists = kb_ref[me * LH + h]
        hit = key_block == lists[:, 0:1]
        for s in range(1, 16):
            hit = hit | (key_block == lists[:, s : s + 1])
        row = jnp.where(hit, 0.0, -jnp.inf).astype(jnp.float32)
        for s in range(SEQ):
            bias[h, s] = row[2 * s : 2 * s + 2]

    pl.semaphore_wait(barrier, len(targets))

    def remote(src, dst, ssem, rsem, dev):
        return pltpu.make_async_remote_copy(
            src_ref=src, dst_ref=dst, send_sem=ssem, recv_sem=rsem, device_id=dev, device_id_type=MESH
        )

    in_copies = []
    for a, (src, dst) in enumerate(((q_ref, qg), (k_ref, kg), (v_ref, vg))):
        for i, p in enumerate(peers):
            n = a * 7 + i
            in_copies.append(remote(src.at[:, cols(p)], dst.at[me], in_send.at[n], in_recv.at[n], (dp, p)))
    for c in in_copies:
        c.start()

    w_copies = []
    for d in range(1, ZN):
        w_copies.append(
            remote(w_ref, wbuf.at[quad, z], w_send.at[d - 1], w_recv.at[d - 1], (z_at(d) * 4 + quad, me))
        )
    for c in w_copies:
        c.start()

    lo, hi = pl.ds(0, HALF), pl.ds(HALF, HALF)
    up, down, across = (dp, seq_at(0, 1)), (dp, seq_at(0, 3)), (dp, seq_at(1, 0))
    order = [(0, 0), (0, 3), (0, 1), (1, 0), (0, 2), (1, 3), (1, 1), (1, 2)]
    slot_of = {o: seq_at(*o) for o in order}

    def sem_of(dx, dy, half):
        return (order.index((dx % 2, dy % 4)) - 1) * 2 + half

    g_copies = {}

    def pass_on(dx, dy, half, way):
        dev, tdx, tdy = {"up": (up, dx, dy - 1), "down": (down, dx, dy + 1), "across": (across, dx + 1, dy)}[way]
        rows = hi if half else lo
        n = sem_of(tdx, tdy, half)
        src = gall.at[slot_of[(dx % 2, dy % 4)], rows]
        if (dx, dy) == (0, 0):
            src = g_ref.at[rows]
        c = remote(src, gall.at[slot_of[(dx % 2, dy % 4)], rows], g_send.at[n], g_recv.at[n], dev)
        c.start()
        g_copies[n] = c

    done = set()

    def arrived(dx, dy, half):
        n = sem_of(dx, dy, half)
        if n not in done:
            done.add(n)
            g_copies[n].wait_recv()

    for half in (0, 1):
        pass_on(0, 0, half, "across")
        pass_on(0, 0, half, "up")
        pass_on(0, 0, half, "down")

    for c in local:
        c.wait()
    for c in in_copies:
        c.wait_recv()

    def head_cols(h):
        return pl.ds(pl.multiple_of(h * HD, HD), HD)

    scale = HD ** -0.5

    def forward(n, carry):
        s = n // LH
        h = n % LH
        hc = head_cols(h)
        query = qg[s, :, hc]
        key = kg[:, :, hc].reshape(LEN, HD)
        value = vg[:, :, hc].reshape(LEN, HD)
        scores = dot_nt(query, key) * (scale * LOG2E)
        b = bias[h, s]
        mask = jnp.concatenate(
            (jnp.broadcast_to(b[0:1], (BLK, LEN)), jnp.broadcast_to(b[1:2], (BLK, LEN))), axis=0
        )
        scores = scores + mask
        expo = jnp.exp2(scores - jnp.max(scores, axis=-1, keepdims=True))
        p = expo * (1.0 / jnp.sum(expo, axis=-1, keepdims=True))
        probs[h, s] = p
        outs[s, :, hc] = dot_nn(p.astype(jnp.bfloat16), value).astype(jnp.bfloat16)
        return carry

    def relay_first():
        arrived(0, 3, 0)
        pass_on(0, 3, 0, "up")
        pass_on(0, 3, 0, "across")
        arrived(0, 1, 1)
        pass_on(0, 1, 1, "down")
        pass_on(0, 1, 1, "across")
        arrived(1, 0, 0)
        pass_on(1, 0, 0, "down")
        arrived(1, 0, 1)
        pass_on(1, 0, 1, "up")

    def relay_second():
        arrived(1, 3, 0)
        pass_on(1, 3, 0, "up")
        arrived(1, 1, 1)
        pass_on(1, 1, 1, "down")

    lax.fori_loop(0, SEQ * LH, forward, 0)

    for c in w_copies:
        c.wait_recv()
    plane_mate = remote(wbuf.at[quad], wbuf.at[quad], w_send.at[15], w_recv.at[15], (mate, me))
    plane_side = remote(wbuf.at[quad], wbuf.at[quad], w_send.at[16], w_recv.at[16], (side, me))
    plane_mate.start()
    plane_side.start()
    relay_first()
    plane_side.wait_recv()
    far = (1 - xl) * 2 + core
    plane_far = remote(wbuf.at[far], wbuf.at[far], w_send.at[17], w_recv.at[17], (mate, me))
    plane_far.start()
    plane_mate.wait_recv()
    plane_far.wait_recv()

    def assemble(i, carry):
        group = jnp.concatenate([wbuf[q, i].astype(jnp.float32) for q in range(4)], axis=0)
        wt[pl.ds(pl.multiple_of(i * 4 * OWN, 32), 4 * OWN), :] = group.astype(jnp.bfloat16)
        return carry

    lax.fori_loop(0, ZN, assemble, 0)

    o_copies = []

    def backward(step):
        slot = slot_of[order[step]]
        grad_heads = dot_nn(gall[slot], wt[...]).astype(jnp.bfloat16)
        dqb[slot] = grad_heads

        def one_head(h, carry):
            hc = head_cols(h)
            key = kg[:, :, hc].reshape(LEN, HD)
            value = vg[:, :, hc].reshape(LEN, HD)
            dprob = dot_nt(dqb[slot, :, hc], value)
            p = probs[h, slot]
            delta = jnp.sum(p * dprob, axis=-1, keepdims=True)
            dscore = (p * (dprob - delta) * scale).astype(jnp.bfloat16)
            dqb[slot, :, hc] = dot_nn(dscore, key).astype(jnp.bfloat16)
            part = dot_tn(dscore, qg[slot, :, hc])
            if step == 0:
                dkacc[h] = part
            else:
                dkacc[h] += part
            return carry

        lax.fori_loop(0, LH, one_head, 0)
        if step == 0:
            c = pltpu.make_async_copy(dqb.at[slot], dq_out.at[:, cols(me)], loc.at[5])
        else:
            c = remote(
                dqb.at[slot], dq_out.at[:, cols(me)], o_send.at[step - 1], o_recv.at[step - 1], (dp, slot)
            )
        c.start()
        o_copies.append(c)

    backward(0)
    for step in range(1, SEQ):
        if step == 1:
            relay_second()
        for half in (0, 1):
            arrived(*order[step], half)
        backward(step)

    def weight_rows(i, carry):
        cc = pl.ds(pl.multiple_of(i * 512, 512), 512)
        part = dot_tn(gall[:, :, cc].reshape(LEN, 512), outs[...].reshape(LEN, LW))
        gw[cc, :] = part
        return carry

    lax.fori_loop(0, CW // 512, weight_rows, 0)

    def spread(i, carry):
        for q in range(4):
            rows = pl.ds(pl.multiple_of(i * 4 * OWN + q * OWN, 8), OWN)
            rsrc[q, i] = gw[rows, :].astype(jnp.bfloat16)
        return carry

    lax.fori_loop(0, ZN, spread, 0)

    other = 1 - core
    pair = [
        remote(rsrc.at[x * 2 + other], r1.at[x], r_send.at[x], r_recv.at[x], (mate, me)) for x in range(2)
    ]
    for c in pair:
        c.start()

    for h in range(LH):
        dkb[:, :, h * HD : (h + 1) * HD] = dkacc[h].astype(jnp.bfloat16).reshape(SEQ, ROWS, HD)
    k_copies = [pltpu.make_async_copy(dkb.at[me], dk_out.at[:, cols(me)], loc.at[6])]
    for step in range(1, SEQ):
        slot = slot_of[order[step]]
        n = 6 + step
        k_copies.append(remote(dkb.at[slot], dk_out.at[:, cols(me)], o_send.at[n], o_recv.at[n], (dp, slot)))
    for c in k_copies:
        c.start()

    for c in pair:
        c.wait_recv()

    def add_side(i, carry):
        t1[i] = (rsrc[(1 - xl) * 2 + core, i].astype(jnp.float32) + r1[1 - xl, i].astype(jnp.float32)).astype(
            jnp.bfloat16
        )
        return carry

    lax.fori_loop(0, ZN, add_side, 0)
    side_copy = remote(t1, r2, r_send.at[2], r_recv.at[2], (side, me))
    side_copy.start()
    side_copy.wait_recv()

    def add_own(i, carry):
        total = rsrc[quad, i].astype(jnp.float32) + r1[xl, i].astype(jnp.float32) + r2[i].astype(jnp.float32)
        t2[i] = total.astype(jnp.bfloat16)
        return carry

    lax.fori_loop(0, ZN, add_own, 0)
    z_copies = []
    for d in range(1, ZN):
        z_copies.append(
            remote(
                t2.at[z_at(d)], r3.at[d - 1], r_send.at[2 + d], r_recv.at[2 + d], (z_at(d) * 4 + quad, me)
            )
        )
    for c in z_copies:
        c.start()
    total = t2[z].astype(jnp.float32)
    for d, c in enumerate(z_copies):
        c.wait_recv()
        total = total + r3[d].astype(jnp.float32)
    dw_out[...] = total

    for c in (o_copies[0], k_copies[0]):
        c.wait()
    for c in o_copies[1:] + k_copies[1:]:
        c.wait()
    for c in in_copies + w_copies + list(g_copies.values()):
        c.wait_send()
    for c in (plane_mate, plane_side, plane_far, pair[0], pair[1], side_copy):
        c.wait_send()
    for c in z_copies:
        c.wait_send()


def per_device(queries, key_states, value_states, grad_out, out_weight, key_blocks, key_count):
    bf, f32 = jnp.bfloat16, jnp.float32
    used = jnp.arange(16)[None, None, :] < key_count[:, :, None]
    lists = jnp.where(used, key_blocks, -1)
    vmem = pl.BlockSpec(memory_space=pltpu.VMEM)
    dma = pltpu.SemaphoreType.DMA
    grad_q, grad_k, grad_w = pl.pallas_call(
        kernel,
        name="bigbird_backward",
        out_shape=(
            jax.ShapeDtypeStruct((ROWS, HEADS * HD), bf),
            jax.ShapeDtypeStruct((ROWS, HEADS * HD), bf),
            jax.ShapeDtypeStruct((OWN, LW), f32),
        ),
        in_specs=[vmem] * 6,
        out_specs=(vmem, vmem, vmem),
        scratch_shapes=[
            pltpu.VMEM((SEQ, ROWS, LW), bf),
            pltpu.VMEM((SEQ, ROWS, LW), bf),
            pltpu.VMEM((SEQ, ROWS, LW), bf),
            pltpu.VMEM((SEQ, ROWS, CW), bf),
            pltpu.VMEM((4, ZN, OWN, LW), bf),
            pltpu.VMEM((CW, LW), bf),
            pltpu.VMEM((LH, SEQ, 2, LEN), f32),
            pltpu.VMEM((LH, SEQ, ROWS, LEN), f32),
            pltpu.VMEM((SEQ, ROWS, LW), bf),
            pltpu.VMEM((SEQ, ROWS, LW), bf),
            pltpu.VMEM((SEQ, ROWS, LW), bf),
            pltpu.VMEM((LH, LEN, HD), f32),
            pltpu.VMEM((CW, LW), f32),
            pltpu.VMEM((4, ZN, OWN, LW), bf),
            pltpu.VMEM((2, ZN, OWN, LW), bf),
            pltpu.VMEM((ZN, OWN, LW), bf),
            pltpu.VMEM((ZN, OWN, LW), bf),
            pltpu.VMEM((ZN, OWN, LW), bf),
            pltpu.VMEM((ZN - 1, OWN, LW), bf),
            dma((21,)), dma((21,)), dma((7,)),
            dma((14,)), dma((14,)),
            dma((18,)), dma((18,)),
            dma((14,)), dma((14,)),
            dma((18,)), dma((18,)),
        ],
        compiler_params=pltpu.CompilerParams(
            collective_id=0, has_side_effects=True, vmem_limit_bytes=60 * 1024 * 1024
        ),
    )(queries, key_states, value_states, grad_out, out_weight.T, lists)
    return grad_q, grad_k, grad_w.T


def solution(mesh):
    return jax.shard_map(
        per_device,
        mesh=mesh,
        in_specs=(
            P(("dp", "seq"), None),
            P(("dp", "seq"), None),
            P(("dp", "seq"), None),
            P(("dp", "seq"), None),
            P("seq", "dp"),
            P(),
            P(),
        ),
        out_specs=(P(("dp", "seq"), None), P(("dp", "seq"), None), P("seq", "dp")),
        check_vma=False,
    )
```

time: 642 us -> 156 us (0.24)
  waiting for transfers between devices: 406 us -> 0 us
  Pallas kernels: 0 us -> 149 us
  matrix products: 126 us -> 0 us
  local copies, waits for them, and re-layouts: 55.3 us -> 5.46 us
  starting transfers between devices: 29.2 us -> 0 us
  between operations: 13.9 us -> 0.66 us
    unnamed x4 -> x0, waiting for transfers between devices: 190 us -> none
    all_gather x2 -> x0, waiting for transfers between devices: 166 us -> none  [the longest x1 94.1 us: per_device(): whole_grad = lax.all_gather(grad_out, 'seq', axis=0, tiled=True)]
    pallas_call x0 -> x1, Pallas kernels: none -> 149 us  [per_device(): pl.pallas_call(kernel, name='bigbird_backward', out_shape=(jax.ShapeDtype...]
    dot_general x32 -> x0, matrix products: 124 us -> none  [the longest x6 39.7 us: backward_rows(): jnp.einsum('rqk,rqd->rkd', dscore, query_rows, preferred_element_type=jnp...]
    all_to_all x5 -> x0, waiting for transfers between devices: 49.6 us -> none  [the longest x1 12.6 us: per_device(): lax.all_to_all(merge_heads(grad_q), 'seq', split_axis=0, concat_axis=1, t...]
    all_to_all x5 -> x0, starting transfers between devices: 29 us -> none  [the longest x1 7.48 us: per_device(): lax.all_to_all(queries, 'seq', split_axis=1, concat_axis=0, tiled=True)]
    reshape x5 -> x0, local copies, waits for them, and re-layouts: 9.56 us -> none  [the longest x1 5.55 us: reduce_grads(): local_sum = local_sum.reshape(local_count * HD, whole_grad.shape[1])]
    gather x6 -> x0, local copies, waits for them, and re-layouts: 8.97 us -> none  [the longest x3 6.28 us: arrange(): mid_values = value_blocks[chosen].reshape(middle, slot_count * BLK, HD)]
  transfers between devices with their start and end apart: 8 -> 0, of which waited for: 8 -> 0; matrix products, arithmetic and copies ran while one was open for 2% -> 0% of each run, Pallas kernels for 0% -> 0%
where the time goes in v1:
time: 156 us
  Pallas kernels  149 us (96%)
  local copies, waits for them, and re-layouts  5.46 us (4%)
    pallas_call x1, Pallas kernels, per_device(): pl.pallas_call(kernel, name='bigbird_backward', out_shape=(jax.ShapeDtype...  149 us
    unnamed x9, local copies, waits for them, and re-layouts  5.46 us

profile of v1, /device:TPU:1, one launch (start us, length us, event | category | flops | bytes accessed | tf_op | source)
XLA Modules:
  0.0 155.6 jit_solution(14942600216955751581)
XLA Ops:
  0.6 0.8 copy.10
  1.4 1.0 copy.11
  2.4 0.8 fusion.kb_ref
  3.2 148.7 %bigbird_backward.1 = (bf16[128,3072]{1,0:T(8,128)(2,1)}, bf16[128,3072]{1,0:T(8,128)(2,1)}, f32[40,384]{1,0:T(8,128)}) custom-call(bf16[128,3072]{1,0:T(8,128)(2,1)} %q_ref.1, bf16[128,3072]{1,0:T(8,128)(2,1)} %k_ref.1, bf16[128,3072]{1,0:T(8,128)(2,1)} %v_ref.1, bf16[128,2560]{1,0:T(8,128)(2,1)} %g_ref.1, bf16[40,384]{1,0:T(8,128)(2,1)} %bitcast.3, ...), custom_call_target="tpu_custom_call" | custom-call | tf_op jit(solution)/shard_map/bigbird_backward/pallas_call | solution.py:347
  152.0 0.0 copy-start
  152.0 2.1 %copy.15 = bf16[128,3072]{1,0:T(8,128)(2,1)} copy(bf16[128,3072]{1,0:T(8,128)(2,1)} %get-tuple-element.12) | data formatting | bytes 1572864
  154.1 0.0 copy-done
  154.1 0.0 copy-start.1
  154.1 0.9 copy.16
  155.0 0.0 copy-done.1
  155.0 0.6 copy.17
Async XLA Ops:
  152.0 2.1 %copy-start = (bf16[128,3072]{1,0:T(8,128)(2,1)S(1)}, bf16[128,3072]{1,0:T(8,128)(2,1)}, u32[]{:S(2)}) copy-start(bf16[128,3072]{1,0:T(8,128)(2,1)} %get-tuple-element.13) | copy-start | bytes 2359300
  154.1 0.9 copy-start.1

commit v2 on v0

v2 whole, which is shorter than its diff:
```python
import jax
import jax.numpy as jnp
from jax import lax
from jax.experimental import pallas as pl
from jax.experimental.pallas import tpu as pltpu
from jax.sharding import PartitionSpec as P

HEADS = 24
HD = 128
BLK = 64
NB = 16
LOG2E = 1.4426950408889634
MESH = pl.DeviceIdType.MESH

SEQ = 8
ROWS = 128
LEN = SEQ * ROWS
LH = HEADS // SEQ
LW = LH * HD
CW = 2560
HALF = ROWS // 2
ZN = 16
OWN = CW // 64
TILE = 512
SUB = 16
CHUNK = 512


def dot_nn(a, b):
    return lax.dot_general(a, b, (((1,), (0,)), ((), ())), preferred_element_type=jnp.float32)


def dot_nt(a, b):
    return lax.dot_general(a, b, (((1,), (1,)), ((), ())), preferred_element_type=jnp.float32)


def dot_tn(a, b):
    return lax.dot_general(a, b, (((0,), (0,)), ((), ())), preferred_element_type=jnp.float32)


def remote(src, dst, ssem, rsem, dev):
    return pltpu.make_async_remote_copy(
        src_ref=src, dst_ref=dst, send_sem=ssem, recv_sem=rsem, device_id=dev, device_id_type=MESH
    )


def kernel(
    q_ref, k_ref, v_ref, g_ref, w_ref, kb_ref, kc_ref,
    dq_out, dk_out, dw_out,
    qg, kg, vg, gall, gturn, wbuf, wt, bias, work, expos, half, outs, wide, inverse, gheads, dqb, dkb,
    rsrc, r1, t1, r2, t2, r3,
    in_send, in_recv, loc, g_send, g_recv, w_send, w_recv, o_send, o_recv, r_send, r_recv,
):
    bf, f32 = jnp.bfloat16, jnp.float32
    dp = lax.axis_index("dp")
    me = lax.axis_index("seq")
    z = dp // 4
    quad = dp % 4
    xl = quad // 2
    core = quad % 2
    xh = me // 4
    y = me % 4

    def seq_at(dx, dy):
        return ((xh + dx) % 2) * 4 + (y + dy) % 4

    order = [(0, 0), (0, 3), (0, 1), (1, 0), (0, 2), (1, 3), (1, 1), (1, 2)]
    slot_of = {o: seq_at(*o) for o in order}
    peers = [slot_of[o] for o in order[1:]]
    mate = (z * 4 + xl * 2 + (1 - core), me)
    side = (z * 4 + (1 - xl) * 2 + core, me)
    along_z = [(((z + d) % ZN) * 4 + quad, me) for d in range(1, ZN)]

    barrier = pltpu.get_barrier_semaphore()
    targets = along_z + [(dp, p) for p in peers] + [mate, side]
    for t in targets:
        pl.semaphore_signal(barrier, inc=1, device_id=t, device_id_type=MESH)

    def cols(p, h):
        return pl.ds(pl.multiple_of(p * LW + h * HD, 128), HD)

    inputs = ((q_ref, qg), (k_ref, kg), (v_ref, vg))
    local = [pltpu.make_async_copy(g_ref, gall.at[me], loc.at[0])]
    local.append(pltpu.make_async_copy(w_ref, wbuf.at[quad, z], loc.at[1]))
    for a, (src, dst) in enumerate(inputs):
        for h in range(LH):
            local.append(pltpu.make_async_copy(src.at[:, cols(me, h)], dst.at[h, me], loc.at[2 + a * LH + h]))
    for c in local:
        c.start()

    key_block = lax.broadcasted_iota(jnp.int32, (NB, LEN), 1) // BLK
    entry = lax.broadcasted_iota(jnp.int32, (NB, 1), 0)
    lane = lax.broadcasted_iota(jnp.int32, (1, HEADS), 1)
    for h in range(LH):
        mine = lane == me * LH + h

        def mask_row(i, carry):
            count = jnp.sum(jnp.where(mine, kc_ref[pl.ds(i, 1), :], 0), axis=1, keepdims=True)
            listed = jnp.sum(jnp.where(mine, kb_ref[i], 0), axis=1, keepdims=True)
            listed = jnp.where(entry < count, listed, -1)
            hit = jnp.where(listed == key_block, 1.0, 0.0).astype(f32)
            found = jnp.max(hit, axis=0, keepdims=True)
            bias[h, i] = jnp.where(found > 0.5, 0.0, -jnp.inf).astype(f32)
            return carry

        lax.fori_loop(0, NB, mask_row, 0)

    pl.semaphore_wait(barrier, len(targets))

    up, down, across = (dp, seq_at(0, 1)), (dp, seq_at(0, 3)), (dp, seq_at(1, 0))

    def sem_of(dx, dy, part):
        return (order.index((dx % 2, dy % 4)) - 1) * 2 + part

    g_copies = {}

    def pass_on(dx, dy, part, way):
        dev, tdx, tdy = {"up": (up, dx, dy - 1), "down": (down, dx, dy + 1), "across": (across, dx + 1, dy)}[way]
        rows = pl.ds(part * HALF, HALF)
        n = sem_of(tdx, tdy, part)
        slot = slot_of[(dx % 2, dy % 4)]
        src = g_ref.at[rows] if (dx, dy) == (0, 0) else gall.at[slot, rows]
        c = remote(src, gall.at[slot, rows], g_send.at[n], g_recv.at[n], dev)
        c.start()
        g_copies[n] = c

    done = set()

    def arrived(dx, dy, part):
        n = sem_of(dx, dy, part)
        if n not in done:
            done.add(n)
            g_copies[n].wait_recv()

    for part in (0, 1):
        pass_on(0, 0, part, "across")
    pass_on(0, 0, 0, "up")
    pass_on(0, 0, 1, "down")
    pass_on(0, 0, 1, "up")
    pass_on(0, 0, 0, "down")

    w_copies = []
    for d in range(1, ZN):
        w_copies.append(remote(w_ref, wbuf.at[quad, z], w_send.at[d - 1], w_recv.at[d - 1], along_z[d - 1]))
    for c in w_copies:
        c.start()

    in_copies = []

    def send_inputs(h):
        for a, (src, dst) in enumerate(inputs):
            for i, p in enumerate(peers):
                n = (h * 3 + a) * 7 + i
                c = remote(src.at[:, cols(p, h)], dst.at[h, me], in_send.at[n], in_recv.at[n], (dp, p))
                c.start()
                in_copies.append(c)

    def turn(step):
        slot = slot_of[order[step]]
        place = pl.ds(pl.multiple_of(slot * ROWS, 128), ROWS)

        def piece(i, carry):
            cc = pl.ds(pl.multiple_of(i * CHUNK, 128), CHUNK)
            gturn[cc, place] = gall[slot, :, cc].T
            return carry

        lax.fori_loop(0, CW // CHUNK, piece, 0)

    def inputs_arrived(h):
        for c in in_copies[h * 21 : (h + 1) * 21]:
            c.wait_recv()

    def assemble(i, carry):
        group = jnp.concatenate([wbuf[q, i].astype(f32) for q in range(4)], axis=0)
        wt[pl.ds(pl.multiple_of(i * 4 * OWN, 32), 4 * OWN), :] = group.astype(bf)
        return carry

    far = (1 - xl) * 2 + core

    def head_gradients(column):
        first = column * 4
        part = dot_nn(gall[pl.ds(first, 4)].reshape(4 * ROWS, CW), wt[...]).astype(bf)
        rows = pl.ds(pl.multiple_of(first * ROWS, 4 * ROWS), 4 * ROWS)
        for h in range(LH):
            gheads[h, rows, :] = part[:, h * HD : (h + 1) * HD]

    scale = HD ** -0.5
    shards = TILE // ROWS

    def forward(h):
        key = kg[h].reshape(LEN, HD)

        def scores(i, carry):
            query = qg[h, pl.ds(i * shards, shards)].reshape(TILE, HD)
            work[pl.ds(pl.multiple_of(i * TILE, TILE), TILE), :] = dot_nt(query, key)
            return carry

        lax.fori_loop(0, LEN // TILE, scores, 0)

        def softmax(i, carry):
            mask = bias[h, i]
            for j in range(BLK // SUB):
                rows = pl.ds(pl.multiple_of(i * BLK + j * SUB, SUB), SUB)
                s = work[rows, :] * (scale * LOG2E) + mask
                expo = jnp.exp2(s - jnp.max(s, axis=-1, keepdims=True))
                inverse[h % 2, rows, :] = 1.0 / jnp.sum(expo, axis=-1, keepdims=True)
                expos[h % 2, rows, :] = expo
                half[rows, :] = expo.astype(bf)
            return carry

        lax.fori_loop(0, NB, softmax, 0)

        def mix(i, carry):
            rows = pl.ds(pl.multiple_of(i * TILE, TILE), TILE)
            part = dot_nn(half[rows, :], vg[h].reshape(LEN, HD)) * inverse[h % 2, rows, :]
            wide[h % 2, rows, :] = part
            outs[rows, h * HD : (h + 1) * HD] = part.astype(bf)
            return carry

        lax.fori_loop(0, LEN // TILE, mix, 0)

    def weight_gradient(first, count):
        group = CW // 4
        mine = slice(first * HD, (first + count) * HD)

        def product(i, carry):
            part = dot_nn(gturn[pl.ds(pl.multiple_of(i * group, 128), group), :], outs[:, mine])
            for n in range(count):
                one = part[:, n * HD : (n + 1) * HD].reshape(4, 4, OWN, HD).astype(bf)
                for q in range(4):
                    rsrc[first + n, q, pl.ds(i * 4, 4)] = one[:, q]
            return carry

        lax.fori_loop(0, 4, product, 0)

    pair, sides, zs = {}, {}, {}

    def sum_pair(h):
        pair[h] = [
            remote(
                rsrc.at[h, x * 2 + 1 - core], r1.at[h, x], r_send.at[h * 18 + x], r_recv.at[h * 18 + x], mate
            )
            for x in range(2)
        ]
        for c in pair[h]:
            c.start()

    def sum_side(h):
        for c in pair[h]:
            c.wait_recv()

        def add(i, carry):
            t1[h, i] = (rsrc[h, far, i].astype(f32) + r1[h, 1 - xl, i].astype(f32)).astype(bf)
            return carry

        lax.fori_loop(0, ZN, add, 0)
        sides[h] = remote(t1.at[h], r2.at[h], r_send.at[h * 18 + 2], r_recv.at[h * 18 + 2], side)
        sides[h].start()

    def sum_z(h):
        sides[h].wait_recv()

        def add(i, carry):
            t2[h, i] = (rsrc[h, quad, i].astype(f32) + r1[h, xl, i].astype(f32) + r2[h, i].astype(f32)).astype(bf)
            return carry

        lax.fori_loop(0, ZN, add, 0)
        zs[h] = []
        for d in range(1, ZN):
            n = h * 18 + 2 + d
            zs[h].append(
                remote(t2.at[h, (z + d) % ZN], r3.at[h, d - 1], r_send.at[n], r_recv.at[n], along_z[d - 1])
            )
        for c in zs[h]:
            c.start()

    def sum_last(h):
        total = t2[h, z].astype(f32)
        for d, c in enumerate(zs[h]):
            c.wait_recv()
            total = total + r3[h, d].astype(f32)
        dw_out[:, h * HD : (h + 1) * HD] = total

    o_copies = []

    def send_back(h, a, src, dst):
        c = pltpu.make_async_copy(src.at[h, me], dst.at[:, cols(me, h)], loc.at[11 + h * 2 + a])
        c.start()
        o_copies.append((True, c))
        for i, p in enumerate(peers):
            n = (h * 2 + a) * 7 + i
            c = remote(src.at[h, p], dst.at[:, cols(me, h)], o_send.at[n], o_recv.at[n], (dp, p))
            c.start()
            o_copies.append((False, c))

    def backward(h, between):
        key = kg[h].reshape(LEN, HD)
        value = vg[h].reshape(LEN, HD)

        def products(i, carry):
            rows = pl.ds(pl.multiple_of(i * TILE, TILE), TILE)
            work[rows, :] = dot_nt(gheads[h, rows, :], value)
            return carry

        lax.fori_loop(0, LEN // TILE, products, 0)

        def softmax_grad(i, carry):
            for j in range(BLK // SUB):
                rows = pl.ds(pl.multiple_of(i * BLK + j * SUB, SUB), SUB)
                delta = jnp.sum(wide[h % 2, rows, :] * gheads[h, rows, :].astype(f32), axis=-1, keepdims=True)
                factor = inverse[h % 2, rows, :] * scale
                half[rows, :] = (expos[h % 2, rows, :] * ((work[rows, :] - delta) * factor)).astype(bf)
            return carry

        lax.fori_loop(0, NB, softmax_grad, 0)
        between()

        def query_grad(i, carry):
            rows = pl.ds(pl.multiple_of(i * TILE, TILE), TILE)
            part = dot_nn(half[rows, :], key).astype(bf)
            dqb[h, pl.ds(i * shards, shards)] = part.reshape(shards, ROWS, HD)
            return carry

        lax.fori_loop(0, LEN // TILE, query_grad, 0)
        send_back(h, 0, dqb, dq_out)

        def key_grad(i, carry):
            rows = pl.ds(pl.multiple_of(i * TILE, TILE), TILE)
            part = dot_tn(half[:, rows], qg[h].reshape(LEN, HD)).astype(bf)
            dkb[h, pl.ds(i * shards, shards)] = part.reshape(shards, ROWS, HD)
            return carry

        lax.fori_loop(0, LEN // TILE, key_grad, 0)
        send_back(h, 1, dkb, dk_out)

    send_inputs(0)
    send_inputs(1)
    arrived(0, 3, 0)
    pass_on(0, 3, 0, "up")
    pass_on(0, 3, 0, "across")
    arrived(0, 1, 1)
    pass_on(0, 1, 1, "down")
    pass_on(0, 1, 1, "across")
    arrived(1, 0, 0)
    pass_on(1, 0, 0, "down")
    arrived(1, 0, 1)
    pass_on(1, 0, 1, "up")
    for c in local:
        c.wait()
    turn(0)
    inputs_arrived(0)
    forward(0)

    for c in w_copies:
        c.wait_recv()
    plane = [
        remote(wbuf.at[quad], wbuf.at[quad], w_send.at[15], w_recv.at[15], mate),
        remote(wbuf.at[quad], wbuf.at[quad], w_send.at[16], w_recv.at[16], side),
    ]
    for c in plane:
        c.start()
    inputs_arrived(1)
    forward(1)
    arrived(1, 3, 0)
    pass_on(1, 3, 0, "up")
    arrived(1, 1, 1)
    pass_on(1, 1, 1, "down")
    send_inputs(2)
    for step in range(1, 5):
        for part in (0, 1):
            arrived(*order[step], part)
        turn(step)
    plane[1].wait_recv()
    plane.append(remote(wbuf.at[far], wbuf.at[far], w_send.at[17], w_recv.at[17], mate))
    plane[2].start()
    plane[0].wait_recv()
    plane[2].wait_recv()
    lax.fori_loop(0, ZN, assemble, 0)
    head_gradients(xh)
    for step in range(5, SEQ):
        for part in (0, 1):
            arrived(*order[step], part)
        turn(step)
    weight_gradient(0, 2)
    sum_pair(0)
    sum_pair(1)
    head_gradients(1 - xh)
    backward(0, lambda: None)
    sum_side(0)
    sum_side(1)
    backward(1, lambda: None)
    inputs_arrived(2)
    forward(2)
    weight_gradient(2, 1)
    sum_pair(2)
    sum_z(0)
    sum_z(1)
    backward(2, lambda: sum_side(2))
    sum_last(0)
    sum_z(2)
    sum_last(1)
    sum_last(2)

    for here, c in o_copies:
        c.wait()
    for c in in_copies + w_copies + plane + list(g_copies.values()):
        c.wait_send()
    for h in range(LH):
        for c in pair[h] + [sides[h]] + zs[h]:
            c.wait_send()


def per_device(queries, key_states, value_states, grad_out, out_weight, key_blocks, key_count):
    bf, f32 = jnp.bfloat16, jnp.float32
    vmem = pl.BlockSpec(memory_space=pltpu.VMEM)
    dma = pltpu.SemaphoreType.DMA
    head_rows = pltpu.VMEM((LH, SEQ, ROWS, HD), bf)
    grad_q, grad_k, grad_w = pl.pallas_call(
        kernel,
        name="bigbird_backward",
        out_shape=(
            jax.ShapeDtypeStruct((ROWS, HEADS * HD), bf),
            jax.ShapeDtypeStruct((ROWS, HEADS * HD), bf),
            jax.ShapeDtypeStruct((OWN, LW), f32),
        ),
        in_specs=[vmem] * 7,
        out_specs=(vmem, vmem, vmem),
        scratch_shapes=[
            head_rows, head_rows, head_rows,
            pltpu.VMEM((SEQ, ROWS, CW), bf),
            pltpu.VMEM((CW, LEN), bf),
            pltpu.VMEM((4, ZN, OWN, LW), bf),
            pltpu.VMEM((CW, LW), bf),
            pltpu.VMEM((LH, NB, 1, LEN), f32),
            pltpu.VMEM((LEN, LEN), f32),
            pltpu.VMEM((2, LEN, LEN), f32),
            pltpu.VMEM((LEN, LEN), bf),
            pltpu.VMEM((LEN, LW), bf),
            pltpu.VMEM((2, LEN, HD), f32),
            pltpu.VMEM((2, LEN, 1), f32),
            pltpu.VMEM((LH, LEN, HD), bf),
            head_rows, head_rows,
            pltpu.VMEM((LH, 4, ZN, OWN, HD), bf),
            pltpu.VMEM((LH, 2, ZN, OWN, HD), bf),
            pltpu.VMEM((LH, ZN, OWN, HD), bf),
            pltpu.VMEM((LH, ZN, OWN, HD), bf),
            pltpu.VMEM((LH, ZN, OWN, HD), bf),
            pltpu.VMEM((LH, ZN - 1, OWN, HD), bf),
            dma((63,)), dma((63,)), dma((17,)),
            dma((14,)), dma((14,)),
            dma((18,)), dma((18,)),
            dma((42,)), dma((42,)),
            dma((54,)), dma((54,)),
        ],
        compiler_params=pltpu.CompilerParams(
            collective_id=0, has_side_effects=True, vmem_limit_bytes=60 * 1024 * 1024
        ),
    )(queries, key_states, value_states, grad_out, out_weight.T, key_blocks.transpose(1, 2, 0), key_count.T)
    return grad_q, grad_k, grad_w.T


def solution(mesh):
    return jax.shard_map(
        per_device,
        mesh=mesh,
        in_specs=(
            P(("dp", "seq"), None),
            P(("dp", "seq"), None),
            P(("dp", "seq"), None),
            P(("dp", "seq"), None),
            P("seq", "dp"),
            P(),
            P(),
        ),
        out_specs=(P(("dp", "seq"), None), P(("dp", "seq"), None), P("seq", "dp")),
        check_vma=False,
    )
```

time: 642 us -> 137 us (0.21)
  waiting for transfers between devices: 406 us -> 0 us
  Pallas kernels: 0 us -> 133 us
  matrix products: 126 us -> 0 us
  local copies, waits for them, and re-layouts: 55.3 us -> 3.65 us
  starting transfers between devices: 29.2 us -> 0 us
  between operations: 13.9 us -> 0.65 us
    unnamed x4 -> x0, waiting for transfers between devices: 190 us -> none
    all_gather x2 -> x0, waiting for transfers between devices: 166 us -> none  [the longest x1 94.1 us: per_device(): whole_grad = lax.all_gather(grad_out, 'seq', axis=0, tiled=True)]
    pallas_call x0 -> x1, Pallas kernels: none -> 133 us  [per_device(): pl.pallas_call(kernel, name='bigbird_backward', out_shape=(jax.ShapeDtype...]
    dot_general x32 -> x0, matrix products: 124 us -> none  [the longest x6 39.7 us: backward_rows(): jnp.einsum('rqk,rqd->rkd', dscore, query_rows, preferred_element_type=jnp...]
    all_to_all x5 -> x0, waiting for transfers between devices: 49.6 us -> none  [the longest x1 12.6 us: per_device(): lax.all_to_all(merge_heads(grad_q), 'seq', split_axis=0, concat_axis=1, t...]
    all_to_all x5 -> x0, starting transfers between devices: 29 us -> none  [the longest x1 7.48 us: per_device(): lax.all_to_all(queries, 'seq', split_axis=1, concat_axis=0, tiled=True)]
    reshape x5 -> x0, local copies, waits for them, and re-layouts: 9.56 us -> none  [the longest x1 5.55 us: reduce_grads(): local_sum = local_sum.reshape(local_count * HD, whole_grad.shape[1])]
    gather x6 -> x0, local copies, waits for them, and re-layouts: 8.97 us -> none  [the longest x3 6.28 us: arrange(): mid_values = value_blocks[chosen].reshape(middle, slot_count * BLK, HD)]
  transfers between devices with their start and end apart: 8 -> 0, of which waited for: 8 -> 0; matrix products, arithmetic and copies ran while one was open for 2% -> 0% of each run, Pallas kernels for 0% -> 0%
where the time goes in v2:
time: 137 us
  Pallas kernels  133 us (97%)
  local copies, waits for them, and re-layouts  3.65 us (3%)
    pallas_call x1, Pallas kernels, per_device(): pl.pallas_call(kernel, name='bigbird_backward', out_shape=(jax.ShapeDtype...  133 us
    unnamed x7, local copies, waits for them, and re-layouts  3.65 us

profile of v2, /device:TPU:1, one launch (start us, length us, event | category | flops | bytes accessed | tf_op | source)
XLA Modules:
  0.0 137.0 jit_solution(2237619980743336516)
XLA Ops:
  0.6 132.7 %bigbird_backward.1 = (bf16[128,3072]{1,0:T(8,128)(2,1)}, bf16[128,3072]{1,0:T(8,128)(2,1)}, f32[40,384]{1,0:T(8,128)}) custom-call(bf16[128,3072]{1,0:T(8,128)(2,1)} %q_ref.1, bf16[128,3072]{1,0:T(8,128)(2,1)} %k_ref.1, bf16[128,3072]{1,0:T(8,128)(2,1)} %v_ref.1, bf16[128,2560]{1,0:T(8,128)(2,1)} %g_ref.1, bf16[40,384]{1,0:T(8,128)(2,1)} %bitcast.6, ...), custom_call_target="tpu_custom_call" | custom-call | tf_op jit(solution)/shard_map/bigbird_backward/pallas_call | solution.py:418
  133.4 0.0 copy-start
  133.4 2.1 %copy.13 = bf16[128,3072]{1,0:T(8,128)(2,1)} copy(bf16[128,3072]{1,0:T(8,128)(2,1)} %get-tuple-element.12) | data formatting | bytes 1572864
  135.5 0.0 copy-done
  135.5 0.0 copy-start.1
  135.5 0.9 copy.14
  136.4 0.0 copy-done.1
  136.4 0.6 copy.15
Async XLA Ops:
  133.4 2.1 %copy-start = (bf16[128,3072]{1,0:T(8,128)(2,1)S(1)}, bf16[128,3072]{1,0:T(8,128)(2,1)}, u32[]{:S(2)}) copy-start(bf16[128,3072]{1,0:T(8,128)(2,1)} %get-tuple-element.13) | copy-start | bytes 2359300
  135.5 0.9 copy-start.1

commit v3 on v2

--- a/solution.py
+++ b/solution.py
@@ -388,16 +388,15 @@
     backward(0, lambda: None)
     sum_side(0)
     sum_side(1)
-    backward(1, lambda: None)
     inputs_arrived(2)
     forward(2)
     weight_gradient(2, 1)
     sum_pair(2)
     sum_z(0)
     sum_z(1)
-    backward(2, lambda: sum_side(2))
+    backward(1, lambda: sum_side(2))
+    backward(2, lambda: sum_z(2))
     sum_last(0)
-    sum_z(2)
     sum_last(1)
     sum_last(2)
 

time: 137 us -> 134 us (0.978)
  Pallas kernels: 133 us -> 130 us
    pallas_call x1, Pallas kernels: 133 us -> 130 us  [per_device(): pl.pallas_call(kernel, name='bigbird_backward', out_shape=(jax.ShapeDtype...]
where the time goes in v3:
time: 134 us
  Pallas kernels  130 us (97%)
  local copies, waits for them, and re-layouts  3.65 us (3%)
    pallas_call x1, Pallas kernels, per_device(): pl.pallas_call(kernel, name='bigbird_backward', out_shape=(jax.ShapeDtype...  130 us
    unnamed x7, local copies, waits for them, and re-layouts  3.65 us

profile of v3, /device:TPU:1, one launch (start us, length us, event | category | flops | bytes accessed | tf_op | source)
XLA Modules:
  0.0 134.3 jit_solution(15274531311991170565)
XLA Ops:
  0.6 130.0 %bigbird_backward.1 = (bf16[128,3072]{1,0:T(8,128)(2,1)}, bf16[128,3072]{1,0:T(8,128)(2,1)}, f32[40,384]{1,0:T(8,128)}) custom-call(bf16[128,3072]{1,0:T(8,128)(2,1)} %q_ref.1, bf16[128,3072]{1,0:T(8,128)(2,1)} %k_ref.1, bf16[128,3072]{1,0:T(8,128)(2,1)} %v_ref.1, bf16[128,2560]{1,0:T(8,128)(2,1)} %g_ref.1, bf16[40,384]{1,0:T(8,128)(2,1)} %bitcast.6, ...), custom_call_target="tpu_custom_call" | custom-call | tf_op jit(solution)/shard_map/bigbird_backward/pallas_call | solution.py:417
  130.6 0.0 copy-start
  130.6 2.1 %copy.13 = bf16[128,3072]{1,0:T(8,128)(2,1)} copy(bf16[128,3072]{1,0:T(8,128)(2,1)} %get-tuple-element.12) | data formatting | bytes 1572864
  132.8 0.0 copy-done
  132.8 0.0 copy-start.1
  132.8 0.9 copy.14
  133.7 0.0 copy-done.1
  133.7 0.6 copy.15
Async XLA Ops:
  130.6 2.1 %copy-start = (bf16[128,3072]{1,0:T(8,128)(2,1)S(1)}, bf16[128,3072]{1,0:T(8,128)(2,1)}, u32[]{:S(2)}) copy-start(bf16[128,3072]{1,0:T(8,128)(2,1)} %get-tuple-element.13) | copy-start | bytes 2359300
  132.8 0.9 copy-start.1

commit v4 on v3

--- a/solution.py
+++ b/solution.py
@@ -385,15 +385,15 @@
     sum_pair(0)
     sum_pair(1)
     head_gradients(1 - xh)
-    backward(0, lambda: None)
     sum_side(0)
     sum_side(1)
+    backward(0, lambda: None)
     inputs_arrived(2)
+    sum_z(0)
     forward(2)
+    sum_z(1)
     weight_gradient(2, 1)
     sum_pair(2)
-    sum_z(0)
-    sum_z(1)
     backward(1, lambda: sum_side(2))
     backward(2, lambda: sum_z(2))
     sum_last(0)

time: 134 us -> 130 us (0.970)
  Pallas kernels: 130 us -> 125 us
    pallas_call x1, Pallas kernels: 130 us -> 125 us  [per_device(): pl.pallas_call(kernel, name='bigbird_backward', out_shape=(jax.ShapeDtype...]
where the time goes in v4:
time: 130 us; the launch traced here: 129 us
  Pallas kernels  125 us (96%)
  local copies, waits for them, and re-layouts  3.65 us (3%)
    pallas_call x1, Pallas kernels, per_device(): pl.pallas_call(kernel, name='bigbird_backward', out_shape=(jax.ShapeDtype...  125 us
    unnamed x7, local copies, waits for them, and re-layouts  3.65 us

profile of v4, /device:TPU:1, one launch (start us, length us, event | category | flops | bytes accessed | tf_op | source)
XLA Modules:
  0.0 129.5 jit_solution(12380658337775582458)
XLA Ops:
  0.6 125.2 %bigbird_backward.1 = (bf16[128,3072]{1,0:T(8,128)(2,1)}, bf16[128,3072]{1,0:T(8,128)(2,1)}, f32[40,384]{1,0:T(8,128)}) custom-call(bf16[128,3072]{1,0:T(8,128)(2,1)} %q_ref.1, bf16[128,3072]{1,0:T(8,128)(2,1)} %k_ref.1, bf16[128,3072]{1,0:T(8,128)(2,1)} %v_ref.1, bf16[128,2560]{1,0:T(8,128)(2,1)} %g_ref.1, bf16[40,384]{1,0:T(8,128)(2,1)} %bitcast.6, ...), custom_call_target="tpu_custom_call" | custom-call | tf_op jit(solution)/shard_map/bigbird_backward/pallas_call | solution.py:417
  125.8 0.0 copy-start
  125.8 2.1 %copy.13 = bf16[128,3072]{1,0:T(8,128)(2,1)} copy(bf16[128,3072]{1,0:T(8,128)(2,1)} %get-tuple-element.12) | data formatting | bytes 1572864
  128.0 0.0 copy-done
  128.0 0.0 copy-start.1
  128.0 0.9 copy.14
  128.9 0.0 copy-done.1
  128.9 0.6 copy.15
Async XLA Ops:
  125.8 2.1 %copy-start = (bf16[128,3072]{1,0:T(8,128)(2,1)S(1)}, bf16[128,3072]{1,0:T(8,128)(2,1)}, u32[]{:S(2)}) copy-start(bf16[128,3072]{1,0:T(8,128)(2,1)} %get-tuple-element.13) | copy-start | bytes 2359300
  128.0 0.9 copy-start.1

commit v5 on v4

--- a/solution.py
+++ b/solution.py
@@ -303,6 +303,7 @@
             return carry
 
         lax.fori_loop(0, LEN // TILE, products, 0)
+        between()
 
         def softmax_grad(i, carry):
             for j in range(BLK // SUB):
@@ -313,7 +314,6 @@
             return carry
 
         lax.fori_loop(0, NB, softmax_grad, 0)
-        between()
 
         def query_grad(i, carry):
             rows = pl.ds(pl.multiple_of(i * TILE, TILE), TILE)

time: 130 us -> 129 us (level)
  no operation moved by 1% of the time
where the time goes in v5:
time: 129 us
  Pallas kernels  125 us (97%)
  local copies, waits for them, and re-layouts  3.65 us (3%)
    pallas_call x1, Pallas kernels, per_device(): pl.pallas_call(kernel, name='bigbird_backward', out_shape=(jax.ShapeDtype...  125 us
    unnamed x7, local copies, waits for them, and re-layouts  3.65 us

profile of v5, /device:TPU:1, one launch (start us, length us, event | category | flops | bytes accessed | tf_op | source)
XLA Modules:
  0.0 129.2 jit_solution(8109535609993711969)
XLA Ops:
  0.6 124.9 %bigbird_backward.1 = (bf16[128,3072]{1,0:T(8,128)(2,1)}, bf16[128,3072]{1,0:T(8,128)(2,1)}, f32[40,384]{1,0:T(8,128)}) custom-call(bf16[128,3072]{1,0:T(8,128)(2,1)} %q_ref.1, bf16[128,3072]{1,0:T(8,128)(2,1)} %k_ref.1, bf16[128,3072]{1,0:T(8,128)(2,1)} %v_ref.1, bf16[128,2560]{1,0:T(8,128)(2,1)} %g_ref.1, bf16[40,384]{1,0:T(8,128)(2,1)} %bitcast.6, ...), custom_call_target="tpu_custom_call" | custom-call | tf_op jit(solution)/shard_map/bigbird_backward/pallas_call | solution.py:417
  125.5 0.0 copy-start
  125.5 2.1 %copy.13 = bf16[128,3072]{1,0:T(8,128)(2,1)} copy(bf16[128,3072]{1,0:T(8,128)(2,1)} %get-tuple-element.12) | data formatting | bytes 1572864
  127.7 0.0 copy-done
  127.7 0.0 copy-start.1
  127.7 0.9 copy.14
  128.6 0.0 copy-done.1
  128.6 0.6 copy.15
Async XLA Ops:
  125.5 2.1 %copy-start = (bf16[128,3072]{1,0:T(8,128)(2,1)S(1)}, bf16[128,3072]{1,0:T(8,128)(2,1)}, u32[]{:S(2)}) copy-start(bf16[128,3072]{1,0:T(8,128)(2,1)} %get-tuple-element.13) | copy-start | bytes 2359300
  127.7 0.9 copy-start.1
